TPU v7x, 256 devices: a whole 4x4x8 slice. The times are simulated.
256 devices in a mesh: dp: 8 (over y, z_hi), ctx: 32 (over z_lo, x, core).
Axes of the slice: x: 4, y: 4, z: 8 (z_hi: 2, z_lo: 4; z = z_hi * 4 + z_lo), core: 2. Of those that a mesh axis runs over, the one named last changes fastest.
Arguments:
- layer_input: bfloat16 [8, 4096, 3072], P('dp', 'ctx'), may hold values from -6 to 6
- query_rows: bfloat16 [8, 4096, 3072], P('dp', 'ctx'), may hold values from -6 to 6
- key_rows: bfloat16 [8, 4096, 3072], P('dp', 'ctx'), may hold values from -6 to 6
- value_rows: bfloat16 [8, 4096, 3072], P('dp', 'ctx'), may hold values from -6 to 6
- out_grad: bfloat16 [8, 4096, 3072], P('dp', 'ctx'), may hold values from -6 to 6
Outputs:
- query_grad: bfloat16 [8, 4096, 3072], P('dp', 'ctx')
- key_grad: bfloat16 [8, 4096, 3072], P('dp', 'ctx')
- value_grad: bfloat16 [8, 4096, 3072], P('dp', 'ctx')
- key_weight_grad: float32 [3072, 3072], P('ctx', 'dp')
All inputs are finite; a program needn't handle non-finite values.
Results may differ from a plain program's by a relative error of at most 0.028.
Values may be sent and summed in bfloat16 or wider, within the bound.
A program may use at most 192 MiB of HBM per device.

v0:
```python
import jax
import jax.numpy as jnp
from jax import lax
from jax.sharding import PartitionSpec as P

HEADS = 24
HEAD_DIM = 128


epsilon = 1e-05


def prefix(array, axis, join, neutral, backward):
    count = lax.axis_size(axis)
    place = lax.axis_index(axis)
    ahead = count - 1 - place if backward else place
    gathered = lax.all_gather(array.astype(jnp.bfloat16), axis)
    state = jnp.zeros_like(array) + jnp.asarray(neutral, array.dtype)

    def one(turn, state):
        source = count - 1 - turn if backward else turn
        return join(state, lax.dynamic_index_in_dim(gathered, source, 0, False).astype(array.dtype))

    return lax.fori_loop(0, ahead, one, state)


def feature(values):
    wide = values.astype(jnp.float32)
    return jax.nn.elu(wide) + 1.0


def slope(values):
    wide = values.astype(jnp.float32)
    return jnp.where(wide > 0, 1.0, jnp.exp(jnp.minimum(wide, 0.0)))


def accumulate(earlier, later):
    return earlier + later


def shards(layer_input, query_rows, key_rows, value_rows, out_grad):
    tokens = query_rows.shape[1]
    shaped = (tokens, HEADS, HEAD_DIM)
    query = query_rows[0].reshape(shaped)
    keyed = key_rows[0].reshape(shaped)
    values = value_rows[0].reshape(shaped)
    upstream = out_grad[0].reshape(shaped).astype(jnp.float32)
    query_feature = feature(query).astype(jnp.bfloat16)
    key_feature = feature(keyed).astype(jnp.bfloat16)
    block_state = jnp.einsum(
        "thd,the->hde", key_feature, values, preferred_element_type=jnp.float32
    )
    zero_state = jnp.zeros_like(block_state)
    state_in = prefix(block_state, "ctx", accumulate, zero_state, False).astype(jnp.bfloat16)
    rows_index = lax.broadcasted_iota(jnp.int32, (tokens, tokens), 0)
    cols_index = lax.broadcasted_iota(jnp.int32, (tokens, tokens), 1)
    causal = (cols_index <= rows_index)[None]
    scores = jnp.einsum(
        "thd,shd->hts", query_feature, key_feature, preferred_element_type=jnp.float32
    )
    scores = jnp.where(causal, scores, 0.0).astype(jnp.bfloat16)
    output = jnp.einsum("hts,she->the", scores, values, preferred_element_type=jnp.float32)
    output = output + jnp.einsum(
        "thd,hde->the", query_feature, state_in, preferred_element_type=jnp.float32
    )
    inverse_rms = lax.rsqrt(jnp.mean(output * output, axis=-1, keepdims=True) + epsilon)
    normed = output * inverse_rms
    projection = jnp.mean(upstream * normed, axis=-1, keepdims=True)
    grad_output = (inverse_rms * (upstream - normed * projection)).astype(jnp.bfloat16)
    block_grad = jnp.einsum(
        "thd,the->hde", query_feature, grad_output, preferred_element_type=jnp.float32
    )
    grad_in = prefix(block_grad, "ctx", accumulate, zero_state, True).astype(jnp.bfloat16)
    grad_scores = jnp.einsum(
        "the,she->hts", grad_output, values, preferred_element_type=jnp.float32
    )
    grad_scores = jnp.where(causal, grad_scores, 0.0).astype(jnp.bfloat16)
    query_total = jnp.einsum(
        "hts,shd->thd", grad_scores, key_feature, preferred_element_type=jnp.float32
    )
    query_total = query_total + jnp.einsum(
        "the,hde->thd", grad_output, state_in, preferred_element_type=jnp.float32
    )
    key_total = jnp.einsum(
        "hts,thd->shd", grad_scores, query_feature, preferred_element_type=jnp.float32
    )
    key_total = key_total + jnp.einsum(
        "she,hde->shd", values, grad_in, preferred_element_type=jnp.float32
    )
    value_total = jnp.einsum(
        "hts,the->she", scores, grad_output, preferred_element_type=jnp.float32
    )
    value_total = value_total + jnp.einsum(
        "shd,hde->she", key_feature, grad_in, preferred_element_type=jnp.float32
    )
    key_flat = (key_total * slope(keyed)).astype(jnp.bfloat16).reshape(tokens, -1)
    query_grad = (query_total * slope(query)).astype(jnp.bfloat16).reshape(1, tokens, -1)
    value_grad = value_total.astype(jnp.bfloat16).reshape(1, tokens, -1)
    key_grad = key_flat.reshape(1, tokens, -1)
    input_flat = layer_input[0]
    scale = (lax.axis_size("dp") * lax.axis_size("ctx") * tokens) ** (-0.5)
    contract = (((0,), (0,)), ((), ()))
    by_context = lax.psum_scatter(
        lax.dot_general(key_flat, input_flat, contract, preferred_element_type=jnp.float32).astype(
            jnp.bfloat16
        ),
        "ctx",
        scatter_dimension=0,
        tiled=True,
    )
    summed = lax.psum_scatter(by_context, "dp", scatter_dimension=1, tiled=True).astype(jnp.float32)
    weight_grad = summed * scale
    return (query_grad, key_grad, value_grad, weight_grad)


def solution(mesh):
    placed = (
        P("dp", "ctx", None),
        P("dp", "ctx", None),
        P("dp", "ctx", None),
        P("dp", "ctx", None),
        P("dp", "ctx", None),
    )
    return jax.shard_map(
        shards,
        mesh=mesh,
        in_specs=placed,
        out_specs=(
            P("dp", "ctx", None),
            P("dp", "ctx", None),
            P("dp", "ctx", None),
            P("ctx", "dp"),
        ),
        check_vma=False,
    )
```

profile of v0, /device:TPU:8, one launch (start us, length us, event | category | flops | bytes accessed | tf_op | source)
XLA Modules:
  0.0 685.7 jit_solution(9943859541442904385)
XLA Ops:
  7.2 2.7 copy.29
  10.0 1.5 copy.28
  11.7 1.5 copy-done.7
  13.2 2.7 fusion.2
  17.2 2.5 copy.36
  21.2 1.8 fusion.11
  23.0 139.1 %all-gather.5.cloned.1.call-done = bf16[768,128,128]{2,1,0:T(8,128)(2,1)} async-done(((bf16[24,128,128]{2,1,0:T(8,128)(2,1)}), bf16[768,128,128]{2,1,0:T(8,128)(2,1)}) %all-gather.5.cloned.1.call-update) | async-done | bytes 25165840 | tf_op jit(solution)/shard_map/all_gather | solution.py:17
  162.3 2.7 multiply_reduce_fusion.1
  166.7 1.6 convolution_convert_fusion.1
  168.4 1.8 select_convert_fusion
  172.6 183.5 %all-gather.7.cloned.1.call-done = bf16[768,128,128]{2,1,0:T(8,128)(2,1)} async-done(((bf16[24,128,128]{2,1,0:T(8,128)(2,1)}), bf16[768,128,128]{2,1,0:T(8,128)(2,1)}) %all-gather.7.cloned.1.call-update) | async-done | bytes 25165840 | tf_op jit(solution)/shard_map/all_gather | solution.py:17
  356.2 47.4 %while.23 = (s32[]{:T(128)}, f32[24,128,128]{2,1,0:T(8,128)S(1)}, s32[]{:T(128)}, bf16[32,24,128,128]{3,2,1,0:T(8,128)(2,1)}, s32[]{:T(128)}, /*index=5*/s32[]{:T(128)}, s32[]{:T(128)}, s32[]{:T(128)}) while((s32[]{:T(128)}, f32[24,128,128]{2,1,0:T(8,128)S(1)}, s32[]{:T(128)}, bf16[32,24,128,128]{3,2,1,0:T(8,128)(2,1)}, s32[]{:T(128)}, ...), condition=%wide.region_5.6_spmd, body=%wide.region_4.5_spmd.sunk | while | flops 786438 | bytes 3932303 | solution.py:24
  356.3 1.5 convert_add_fusion.5
  357.8 1.5 convert_add_fusion.5
  359.3 1.5 convert_add_fusion.5
  360.9 1.5 convert_add_fusion.5
  362.4 1.5 convert_add_fusion.5
  363.9 1.5 convert_add_fusion.5
  365.4 1.5 convert_add_fusion.5
  367.0 1.5 convert_add_fusion.5
  368.5 1.5 convert_add_fusion.5
  403.7 2.8 fusion.4
  407.4 9.1 %convolution_convert_fusion = bf16[3072,3072]{1,0:T(8,128)(2,1)} fusion(bf16[128,3072]{0,1:T(8,128)(2,1)S(1)} %bitcast.64, bf16[1,128,3072]{2,1,0:T(8,128)(2,1)S(1)} %copy-done), kind=kOutput, calls=%fused_computation.2 | convolution fusion | flops 2425356288 | bytes 20447232 | tf_op jit(solution)/shard_map/dot_general | solution.py:104
  416.8 175.1 %reduce-scatter.5.cloned.1.call-done = bf16[96,3072]{1,0:T(8,128)(2,1)} async-done(((bf16[3072,3072]{1,0:T(8,128)(2,1)}), bf16[96,3072]{1,0:T(8,128)(2,1)}) %reduce-scatter.5.cloned.1.call-update) | async-done | bytes 589840 | tf_op jit(solution)/shard_map/reduce_scatter | solution.py:103
  591.9 2.3 copy.56
  594.2 2.0 fusion.20
  598.0 2.3 copy.44
  600.3 2.7 fusion.22
  603.0 2.3 copy.45
  605.3 2.8 add_convert_fusion
  608.1 2.3 copy.46
  610.4 67.0 %reduce-scatter.7.cloned.1.call-done = bf16[384,96]{1,0:T(8,128)(2,1)} async-done(((bf16[3072,96]{1,0:T(8,128)(2,1)}), bf16[384,96]{1,0:T(8,128)(2,1)}) %reduce-scatter.7.cloned.1.call-update) | async-done | bytes 73744
  (80 shorter events, 45.1 us)
Async XLA Ops:
  7.2 400.3 %copy-start = (bf16[1,128,3072]{2,1,0:T(8,128)(2,1)S(1)}, bf16[1,128,3072]{2,1,0:T(8,128)(2,1)}, u32[]{:S(2)}) copy-start(bf16[1,128,3072]{2,1,0:T(8,128)(2,1)} %param.9) | copy-start | bytes 2359300
  7.2 2.8 copy-start.17
  7.2 154.9 %all-gather.5.cloned.1.call-start = ((), (), s32[]{:S(2)}) async-start(), calls=%async_computation.3 | async-start | bytes 25952256 | tf_op jit(solution)/shard_map/all_gather | solution.py:17
  10.0 1.5 copy-start.16
  11.5 1.7 copy-start.7
  11.6 8.6 %copy-start.9 = (bf16[16,8,24,128]{3,2,1,0:T(8,128)(2,1)}, bf16[16,8,24,128]{3,2,1,0:T(8,128)(2,1)S(1)}, u32[]{:S(2)}) copy-start(bf16[16,8,24,128]{3,2,1,0:T(8,128)(2,1)S(1)} %copy.58) | copy-start | bytes 2359300
  15.9 3.9 copy-start.4
  17.2 338.9 %all-gather.7.cloned.1.call-start = ((), (), s32[]{:S(2)}) async-start(), calls=%async_computation.4 | async-start | bytes 25952256 | tf_op jit(solution)/shard_map/all_gather | solution.py:17
  20.3 0.9 copy-start.14
  162.3 2.7 copy-start.2
  162.3 2.7 copy-start.6
  165.4 1.3 copy-start.5
  165.8 0.9 copy-start.11
  166.7 1.7 copy-start.10
  168.3 423.6 %reduce-scatter.5.cloned.1.call-start = ((), (), s32[]{:S(2)}) async-start(), calls=%async_computation.2 | async-start | bytes 19464192 | tf_op jit(solution)/shard_map/reduce_scatter | solution.py:103
  170.2 0.9 copy-start.15
  406.5 0.9 copy-start.13
  416.5 260.9 %reduce-scatter.7.cloned.1.call-start = ((), (), s32[]{:S(2)}) async-start(), calls=%async_computation.5 | async-start | bytes 884736
  594.2 2.0 copy-start.12
  594.2 2.0 copy-start.3
  594.2 2.3 copy-start.8
  605.3 73.8 %copy-start.1 = (bf16[1,128,3072]{2,1,0:T(8,128)(2,1)S(1)}, bf16[1,128,3072]{2,1,0:T(8,128)(2,1)}, u32[]{:S(2)}) copy-start(bf16[1,128,3072]{2,1,0:T(8,128)(2,1)} %param.9) | copy-start | bytes 2359300
Sparse Core Ops, SparseCore 0:
  17.3 144.7 all-gather.4
  168.4 187.5 all-gather.6
  416.7 175.1 reduce-scatter.4
  595.6 81.7 reduce-scatter.6
where the time goes:
time: 688 us; the launch traced here: 686 us
  waiting for transfers between devices  565 us (82%)
  other arithmetic  50.7 us (7%)
  matrix products  31.9 us (5%)
  local copies, waits for them, and re-layouts  23 us (3%)
  between operations  14 us (2%)
    all_gather x2, waiting for transfers between devices, prefix(): gathered = lax.all_gather(array.astype(jnp.bfloat16), axis)  323 us
    reduce_scatter x1, waiting for transfers between devices, shards(): lax.psum_scatter(lax.dot_general(key_flat, input_flat, contract, preferre...  175 us
    unnamed x5, waiting for transfers between devices  67.1 us
    add x31, other arithmetic, accumulate(): return earlier + later  46.6 us
    unnamed x42, local copies, waits for them, and re-layouts  15.9 us
  transfers between devices with their start and end apart: 4, of which 4 were waited for; matrix products, arithmetic and copies ran while one was open for 3% of the time, Pallas kernels for 0%

commit v1 on v0

v1 whole, which is shorter than its diff:
```python
import functools

import jax
import jax.numpy as jnp
from jax import lax
from jax.experimental import pallas as pl
from jax.experimental.pallas import tpu as pltpu
from jax.sharding import PartitionSpec as P

HEADS = 24
HD = 128
TOK = 128
HALF = 12
CHIPS = 16
PIECE = 96
WIDE = 3072
EPS = 1e-05
SCALE = (8 * 32 * 128) ** (-0.5)
MESH = pl.DeviceIdType.MESH
F32 = jnp.float32
BF16 = jnp.bfloat16
GROUP = 4

NN = (((1,), (0,)), ((), ()))
NT = (((1,), (1,)), ((), ()))
TN = (((0,), (0,)), ((), ()))


def mm(a, b, dims):
    return lax.dot_general(a, b, dims, preferred_element_type=F32)


def feature(x):
    return jnp.where(x > 0, x + 1.0, jnp.exp(jnp.minimum(x, 0.0)))


def slope(x):
    return jnp.where(x > 0, 1.0, jnp.exp(jnp.minimum(x, 0.0)))


def cols(h):
    return pl.ds(pl.multiple_of(h * HD, HD), HD)


def kernel(
    x_ref, q_ref, k_ref, v_ref, og_ref,
    dq_out, dk_out, dv_out, dw_out,
    qf, kf, go, ol, dkl, dvl, sc,
    st, pb, cs, r1, ex, pr, po, si,
    dq, dk, dv, kgt, xb, at, cp, xr, zs, zr, tb, tr,
    pair_s, pair_r, a2a_s, a2a_r, xb_s, xb_r, at_s, at_r,
    cx_s, cx_r, z_s, z_r, t_s, t_r, loc,
):
    d = lax.axis_index("dp")
    c = lax.axis_index("ctx")
    y, zh = d // 2, d % 2
    chip, core = c // 2, c % 2
    zl, x = chip // 4, chip % 4
    other = 1 - core

    def dev(y_, zh_, zl_, x_, core_):
        return (y_ * 2 + zh_, (zl_ * 4 + x_) * 2 + core_)

    partner = (d, chip * 2 + other)

    def remote(src, dst, ss, rs, to):
        return pltpu.make_async_remote_copy(
            src_ref=src, dst_ref=dst, send_sem=ss, recv_sem=rs,
            device_id=to, device_id_type=MESH,
        )

    barrier = pltpu.get_barrier_semaphore()

    def greet(to):
        pl.semaphore_signal(barrier, inc=1, device_id=to, device_id_type=MESH)

    greet(partner)
    for o in range(1, CHIPS):
        greet((d, ((chip + o) % CHIPS) * 2 + core))
    for o in range(1, 4):
        for cc in (0, 1):
            greet(dev((y + o) % 4, zh, zl, x, cc))
    for o in range(4):
        greet(dev(y, 1 - zh, o, x, core))
    flip = dev(zl, zh, y, x, core)
    off = y != zl

    @pl.when(off)
    def _():
        greet(flip)

    row = lax.broadcasted_iota(jnp.int32, (TOK, TOK), 0)
    col = lax.broadcasted_iota(jnp.int32, (TOK, TOK), 1)
    causal = col <= row

    def heads(first, count, body):
        def step(g, carry):
            for j in range(GROUP):
                body(first + g * GROUP + j)
            return carry

        lax.fori_loop(0, count // GROUP, step, 0)

    def states(h):
        at_h = cols(h)
        kfh = feature(k_ref[:, at_h].astype(F32)).astype(BF16)
        qf[:, at_h] = feature(q_ref[:, at_h].astype(F32)).astype(BF16)
        kf[:, at_h] = kfh
        st[0, h] = mm(kfh, v_ref[:, at_h], TN).astype(BF16)

    heads(HALF * other, HALF, states)

    pl.semaphore_wait(barrier, 26 + ((y - zl) * (y - zl) + 8) // 9)

    def pair_out(s):
        return remote(
            st.at[s, pl.ds(HALF * other, HALF)], pb.at[s],
            pair_s.at[2 * s], pair_r.at[2 * s], partner,
        )

    def pair_back(s):
        return remote(
            po.at[s], si.at[s, pl.ds(HALF * core, HALF)],
            pair_s.at[2 * s + 1], pair_r.at[2 * s + 1], partner,
        )

    def pair_back_in(s):
        return remote(
            po.at[s], si.at[s, pl.ds(HALF * other, HALF)],
            pair_s.at[2 * s + 1], pair_r.at[2 * s + 1], partner,
        )

    def toward(s, o):
        to = (chip + o) % CHIPS
        return remote(
            cs.at[s, pl.ds(PIECE * to, PIECE)], r1.at[s, chip],
            a2a_s.at[2 * s, o], a2a_r.at[2 * s, o], (d, to * 2 + core),
        )

    def toward_in(s, o):
        src = (chip + CHIPS - o) % CHIPS
        return remote(
            cs.at[s, pl.ds(PIECE * src, PIECE)], r1.at[s, src],
            a2a_s.at[2 * s, o], a2a_r.at[2 * s, o], (d, src * 2 + core),
        )

    def away(s, o):
        to = (chip + o) % CHIPS
        return remote(
            ex.at[s, to], pr.at[s, pl.ds(PIECE * chip, PIECE)],
            a2a_s.at[2 * s + 1, o], a2a_r.at[2 * s + 1, o], (d, to * 2 + core),
        )

    def away_in(s, o):
        src = (chip + CHIPS - o) % CHIPS
        return remote(
            ex.at[s, src], pr.at[s, pl.ds(PIECE * src, PIECE)],
            a2a_s.at[2 * s + 1, o], a2a_r.at[2 * s + 1, o], (d, src * 2 + core),
        )

    def scan(s, meanwhile):
        pair_out(s).wait_recv()

        def add(i, carry):
            both = st[s, HALF * core + i].astype(F32) + pb[s, i].astype(F32)
            cs[s, pl.ds(pl.multiple_of(i * HD, HD), HD), :] = both.astype(BF16)
            return carry

        lax.fori_loop(0, HALF, add, 0)
        for o in range(1, CHIPS):
            toward(s, o).start()
        r1[s, chip] = cs[s, pl.ds(pl.multiple_of(PIECE * chip, PIECE), PIECE), :]
        meanwhile()
        for o in range(1, CHIPS):
            toward_in(s, o).wait_recv()
        total = jnp.zeros((PIECE, HD), F32)
        for i in range(CHIPS):
            n = i if s == 0 else CHIPS - 1 - i
            ex[s, n] = total.astype(BF16)
            total = total + r1[s, n].astype(F32)
        for o in range(1, CHIPS):
            away(s, o).start()
        pr[s, pl.ds(pl.multiple_of(PIECE * chip, PIECE), PIECE), :] = ex[s, chip]

    def finish(s):
        for o in range(1, CHIPS):
            away_in(s, o).wait_recv()
        mine_on = (core if s == 0 else 1 - core).astype(F32)
        theirs_on = 1.0 - mine_on

        def theirs(i, carry):
            base = pr[s, pl.ds(pl.multiple_of(i * HD, HD), HD), :].astype(F32)
            po[s, i] = (base + theirs_on * st[s, HALF * core + i].astype(F32)).astype(BF16)
            return carry

        lax.fori_loop(0, HALF, theirs, 0)
        pair_back(s).start()

        def mine(i, carry):
            base = pr[s, pl.ds(pl.multiple_of(i * HD, HD), HD), :].astype(F32)
            si[s, HALF * core + i] = (base + mine_on * pb[s, i].astype(F32)).astype(BF16)
            return carry

        lax.fori_loop(0, HALF, mine, 0)

    slot = 2 * y + core

    def xrows(n):
        return pl.ds(pl.multiple_of(TOK * n, TOK), TOK)

    pair_out(0).start()
    own_x = pltpu.make_async_copy(x_ref, xb.at[xrows(slot)], loc.at[0])
    own_x.start()

    def x_send(o):
        return remote(
            x_ref, xb.at[xrows(slot)], xb_s.at[o], xb_r.at[o],
            dev((y + o) % 4, zh, zl, x, core),
        )

    def x_in(o):
        src = (y + 4 - o) % 4
        return remote(
            x_ref, xb.at[xrows(2 * src + core)], xb_s.at[o], xb_r.at[o],
            dev(src, zh, zl, x, core),
        )

    def x_pass(o):
        src = (y + 4 - o) % 4
        rows = xb.at[xrows(2 * src + core)]
        return remote(rows, rows, xb_s.at[4 + o], xb_r.at[4 + o], partner)

    def x_pass_in(o):
        src = (y + 4 - o) % 4
        rows = xb.at[xrows(2 * src + other)]
        return remote(rows, rows, xb_s.at[4 + o], xb_r.at[4 + o], partner)

    x_keep = remote(x_ref, xb.at[xrows(slot)], xb_s.at[4], xb_r.at[4], partner)
    x_keep_in = remote(x_ref, xb.at[xrows(2 * y + other)], xb_s.at[4], xb_r.at[4], partner)

    for o in (1, 3, 2):
        x_send(o).start()

    heads(HALF * core, HALF, states)

    def local_out(h):
        at_h = cols(h)
        s_h = mm(qf[:, at_h], kf[:, at_h], NT)
        s_h = jnp.where(causal, s_h, 0.0).astype(BF16)
        sc[h] = s_h
        ol[:, at_h] = mm(s_h, v_ref[:, at_h], NN)

    scan(0, lambda: heads(0, HEADS, local_out))
    finish(0)
    x_keep.start()

    def grads(h):
        at_h = cols(h)
        out = ol[:, at_h] + mm(qf[:, at_h], si[0, h], NN)
        inv = lax.rsqrt(jnp.mean(out * out, axis=-1, keepdims=True) + EPS)
        normed = out * inv
        up = og_ref[:, at_h].astype(F32)
        proj = jnp.mean(up * normed, axis=-1, keepdims=True)
        g_h = (inv * (up - normed * proj)).astype(BF16)
        go[:, at_h] = g_h
        st[1, h] = mm(qf[:, at_h], g_h, TN).astype(BF16)

    pair_back_in(0).wait_recv()
    heads(HALF * other, HALF, grads)
    pair_out(1).start()
    heads(HALF * core, HALF, grads)

    def local_grads(h):
        at_h = cols(h)
        g_h = go[:, at_h]
        gs = mm(g_h, v_ref[:, at_h], NT)
        gs = jnp.where(causal, gs, 0.0).astype(BF16)
        total = mm(gs, kf[:, at_h], NN) + mm(g_h, si[0, h], NT)
        dq[:, at_h] = (total * slope(q_ref[:, at_h].astype(F32))).astype(BF16)
        dkl[:, at_h] = mm(gs, qf[:, at_h], TN)
        dvl[:, at_h] = mm(sc[h], g_h, TN)

    def during():
        for o in (1, 3, 2):
            x_in(o).wait_recv()
            x_pass(o).start()
        heads(0, HEADS, local_grads)

    scan(1, during)
    out_q = pltpu.make_async_copy(dq, dq_out, loc.at[1])
    out_q.start()
    finish(1)
    pair_back_in(1).wait_recv()

    def last(h):
        at_h = cols(h)
        gi = si[1, h]
        total = dkl[:, at_h] + mm(v_ref[:, at_h], gi, NT)
        total = total * slope(k_ref[:, at_h].astype(F32))
        dk[:, at_h] = total.astype(BF16)
        kgt[pl.ds(pl.multiple_of(h * HD, HD), HD), :] = total.T.astype(BF16)
        dv[:, at_h] = (dvl[:, at_h] + mm(kf[:, at_h], gi, NN)).astype(BF16)

    heads(0, HEADS, last)

    def at_rows(y_, core_, n):
        return kgt.at[pl.ds(pl.multiple_of(768 * y_ + 192 * n + 96 * core_, 96), 96)]

    def at_put(src, n):
        return at.at[pl.ds(96 * n, 96), pl.ds(pl.multiple_of(TOK * src, TOK), TOK)]

    def at_send(o, cc, n):
        y_ = (y + o) % 4
        cc_ = (core + cc) % 2
        return remote(
            at_rows(y_, cc_, n), at_put(slot, n), at_s.at[2 * o + cc, n], at_r.at[2 * o + cc, n],
            dev(y_, zh, zl, x, cc_),
        )

    def at_in(o, cc, n):
        y_ = (y + 4 - o) % 4
        cc_ = (core + cc) % 2
        return remote(
            at_rows(y, core, n), at_put(2 * y_ + cc_, n), at_s.at[2 * o + cc, n], at_r.at[2 * o + cc, n],
            dev(y_, zh, zl, x, cc_),
        )

    peers = [(o, cc) for o in (2, 1, 3, 0) for cc in (0, 1) if (o, cc) != (0, 0)]
    for o, cc in peers:
        for n in range(4):
            at_send(o, cc, n).start()
    for n in range(4):
        keep = pltpu.make_async_copy(at_rows(y, core, n), at_put(slot, n), loc.at[4 + n])
        keep.start()
    out_k = pltpu.make_async_copy(dk, dk_out, loc.at[2])
    out_v = pltpu.make_async_copy(dv, dv_out, loc.at[3])
    out_k.start()
    out_v.start()

    own_x.wait()
    x_keep_in.wait_recv()
    for o in (1, 3, 2):
        x_pass_in(o).wait_recv()
    for n in range(4):
        pltpu.make_async_copy(at_rows(y, core, n), at_put(slot, n), loc.at[4 + n]).wait()
        for o, cc in peers:
            at_in(o, cc, n).wait_recv()

    def cx_send(o):
        to = (x + o) % 4
        return remote(cp.at[to], xr.at[x], cx_s.at[o], cx_r.at[o], dev(y, zh, zl, to, core))

    def cx_in(o):
        src = (x + 4 - o) % 4
        return remote(cp.at[src], xr.at[src], cx_s.at[o], cx_r.at[o], dev(y, zh, zl, src, core))

    def product(n, carry):
        tile = mm(at[...], xb[:, pl.ds(pl.multiple_of(n * 384, 384), 384)], NN).astype(BF16)
        for i in range(4):
            cp[i, n] = tile[96 * i:96 * (i + 1), :]
        return carry

    lax.fori_loop(0, 8, product, 0)
    for o in (2, 1, 3):
        cx_send(o).start()
    for o in (1, 3, 2):
        cx_in(o).wait_recv()

    def sum_x(n, carry):
        total = cp[x, n].astype(F32)
        for o in range(1, 4):
            total = total + xr[(x + o) % 4, n].astype(F32)
        zs[n] = total.astype(BF16)
        return carry

    lax.fori_loop(0, 8, sum_x, 0)

    z = zh * 4 + zl

    def z_send(o):
        to = (z + o) % 8
        return remote(
            zs.at[(to % 4) * 2 + to // 4], zr.at[o], z_s.at[o], z_r.at[o],
            dev(y, to // 4, to % 4, x, core),
        )

    def z_in(o):
        src = (z + 8 - o) % 8
        return remote(
            zs.at[(src % 4) * 2 + src // 4], zr.at[o], z_s.at[o], z_r.at[o],
            dev(y, src // 4, src % 4, x, core),
        )

    for o in (4, 3, 5, 2, 6, 1, 7):
        z_send(o).start()
    for o in range(1, 8):
        z_in(o).wait_recv()
    total = zs[zl * 2 + zh].astype(F32)
    for o in range(1, 8):
        total = total + zr[o].astype(F32)
    tb[...] = total.astype(BF16)

    turn = remote(tb, tr, t_s.at[0], t_r.at[0], flip)

    @pl.when(off)
    def _():
        turn.start()
        turn.wait()
        dw_out[...] = tr[...].astype(F32) * SCALE

    @pl.when(jnp.logical_not(off))
    def _():
        dw_out[...] = tb[...].astype(F32) * SCALE

    for s in (0, 1):
        pair_out(s).wait_send()
        pair_back(s).wait_send()
        for o in range(1, CHIPS):
            toward(s, o).wait_send()
            away(s, o).wait_send()
    for o in (1, 3, 2):
        x_send(o).wait_send()
        x_pass(o).wait_send()
        cx_send(o).wait_send()
    x_keep.wait_send()
    for o, cc in peers:
        for n in range(4):
            at_send(o, cc, n).wait_send()
    for o in range(1, 8):
        z_send(o).wait_send()
    out_q.wait()
    out_k.wait()
    out_v.wait()


def shards(layer_input, query_rows, key_rows, value_rows, out_grad):
    vmem = pl.BlockSpec(memory_space=pltpu.VMEM)
    hbm = pl.BlockSpec(memory_space=pl.ANY)
    rows = (TOK, WIDE)
    state = (HALF, HD, HD)
    dma = pltpu.SemaphoreType.DMA
    dq, dk, dv, dw = pl.pallas_call(
        kernel,
        out_shape=(
            jax.ShapeDtypeStruct(rows, BF16),
            jax.ShapeDtypeStruct(rows, BF16),
            jax.ShapeDtypeStruct(rows, BF16),
            jax.ShapeDtypeStruct((96, 384), F32),
        ),
        in_specs=[hbm, vmem, vmem, vmem, vmem],
        out_specs=(hbm, hbm, hbm, vmem),
        scratch_shapes=[
            pltpu.VMEM(rows, BF16),
            pltpu.VMEM(rows, BF16),
            pltpu.VMEM(rows, BF16),
            pltpu.VMEM(rows, F32),
            pltpu.VMEM(rows, F32),
            pltpu.VMEM(rows, F32),
            pltpu.VMEM((HEADS, HD, HD), BF16),
            pltpu.VMEM((2, HEADS, HD, HD), BF16),
            pltpu.VMEM((2,) + state, BF16),
            pltpu.VMEM((2, HALF * HD, HD), BF16),
            pltpu.VMEM((2, CHIPS, PIECE, HD), BF16),
            pltpu.VMEM((2, CHIPS, PIECE, HD), BF16),
            pltpu.VMEM((2, HALF * HD, HD), BF16),
            pltpu.VMEM((2,) + state, BF16),
            pltpu.VMEM((2, HEADS, HD, HD), BF16),
            pltpu.VMEM(rows, BF16),
            pltpu.VMEM(rows, BF16),
            pltpu.VMEM(rows, BF16),
            pltpu.VMEM((WIDE, TOK), BF16),
            pltpu.VMEM((8 * TOK, WIDE), BF16),
            pltpu.VMEM((384, 8 * TOK), BF16),
            pltpu.VMEM((4, 8, 96, 384), BF16),
            pltpu.VMEM((4, 8, 96, 384), BF16),
            pltpu.VMEM((8, 96, 384), BF16),
            pltpu.VMEM((8, 96, 384), BF16),
            pltpu.VMEM((96, 384), BF16),
            pltpu.VMEM((96, 384), BF16),
            dma((4,)), dma((4,)),
            dma((4, CHIPS)), dma((4, CHIPS)),
            dma((8,)), dma((8,)),
            dma((8, 4)), dma((8, 4)),
            dma((4,)), dma((4,)),
            dma((8,)), dma((8,)),
            dma((1,)), dma((1,)),
            dma((8,)),
        ],
        compiler_params=pltpu.CompilerParams(
            collective_id=0, has_side_effects=True, vmem_limit_bytes=60 * 1024 * 1024
        ),
    )(layer_input[0], query_rows[0], key_rows[0], value_rows[0], out_grad[0])
    return dq[None], dk[None], dv[None], dw


def solution(mesh):
    placed = (P("dp", "ctx", None),) * 5
    return jax.shard_map(
        shards,
        mesh=mesh,
        in_specs=placed,
        out_specs=(
            P("dp", "ctx", None),
            P("dp", "ctx", None),
            P("dp", "ctx", None),
            P("ctx", "dp"),
        ),
        check_vma=False,
    )
```

time: 688 us -> 138 us (0.20)
  waiting for transfers between devices: 565 us -> 0 us
  Pallas kernels: 0 us -> 132 us
  other arithmetic: 50.7 us -> 0 us
  matrix products: 31.9 us -> 0 us
  local copies, waits for them, and re-layouts: 23 us -> 5.24 us
  between operations: 14 us -> 0.65 us
    all_gather x2 -> x0, waiting for transfers between devices: 323 us -> none  [prefix(): gathered = lax.all_gather(array.astype(jnp.bfloat16), axis)]
    reduce_scatter x1 -> x0, waiting for transfers between devices: 175 us -> none  [shards(): lax.psum_scatter(lax.dot_general(key_flat, input_flat, contract, preferre...]
    pallas_call x0 -> x1, Pallas kernels: none -> 132 us  [shards(): pl.pallas_call(kernel, out_shape=(jax.ShapeDtypeStruct(rows, BF16), jax.S...]
    unnamed x5 -> x0, waiting for transfers between devices: 67.1 us -> none
    add x31 -> x0, other arithmetic: 46.6 us -> none  [accumulate(): return earlier + later]
    dot_general x13 -> x0, matrix products: 31.9 us -> none  [the longest x1 9.07 us: shards(): lax.dot_general(key_flat, input_flat, contract, preferred_element_type=jn...]
    unnamed x42 -> x10, local copies, waits for them, and re-layouts: 15.9 us -> 5.24 us
  transfers between devices with their start and end apart: 4 -> 0, of which waited for: 4 -> 0; matrix products, arithmetic and copies ran while one was open for 3% -> 0% of each run, Pallas kernels for 0% -> 0%
where the time goes in v1:
time: 138 us
  Pallas kernels  132 us (96%)
  local copies, waits for them, and re-layouts  5.24 us (4%)
    pallas_call x1, Pallas kernels, shards(): pl.pallas_call(kernel, out_shape=(jax.ShapeDtypeStruct(rows, BF16), jax.S...  132 us
    unnamed x10, local copies, waits for them, and re-layouts  5.24 us

profile of v1, /device:TPU:8, one launch (start us, length us, event | category | flops | bytes accessed | tf_op | source)
XLA Modules:
  0.0 138.2 jit_solution(2973108881571765633)
XLA Ops:
  0.6 132.3 %shard_map.84 = (bf16[128,3072]{1,0:T(8,128)(2,1)}, bf16[128,3072]{1,0:T(8,128)(2,1)}, bf16[128,3072]{1,0:T(8,128)(2,1)}, f32[96,384]{1,0:T(8,128)}) custom-call(bf16[128,3072]{1,0:T(8,128)(2,1)} %bitcast.11, bf16[128,3072]{1,0:T(8,128)(2,1)} %bitcast.12, bf16[128,3072]{1,0:T(8,128)(2,1)} %bitcast.13, bf16[128,3072]{1,0:T(8,128)(2,1)} %bitcast.14, ...), custom_call_target="tpu_custom_call" | custom-call | tf_op jit(solution)/shard_map/pallas_call | solution.py:442
  133.0 0.0 copy-start.1
  133.0 2.1 %copy.13 = bf16[1,128,3072]{2,1,0:T(8,128)(2,1)} copy(bf16[1,128,3072]{2,1,0:T(8,128)(2,1)} %bitcast.10) | data formatting | bytes 1572864
  135.1 0.0 copy-done.1
  135.1 0.0 copy-start
  135.1 0.9 copy.14
  136.0 0.5 copy-done
  136.5 0.0 copy-start.2
  136.5 0.9 copy.15
  137.4 0.1 copy-done.2
  137.6 0.7 copy.16
Async XLA Ops:
  133.0 2.1 %copy-start.1 = (bf16[128,3072]{1,0:T(8,128)(2,1)S(1)}, bf16[128,3072]{1,0:T(8,128)(2,1)}, u32[]{:S(2)}) copy-start(bf16[128,3072]{1,0:T(8,128)(2,1)} %get-tuple-element.9) | copy-start | bytes 2359300
  135.1 1.4 %copy-start = (bf16[128,3072]{1,0:T(8,128)(2,1)S(1)}, bf16[128,3072]{1,0:T(8,128)(2,1)}, u32[]{:S(2)}) copy-start(bf16[128,3072]{1,0:T(8,128)(2,1)} %get-tuple-element.10) | copy-start | bytes 2359300
  136.5 1.0 copy-start.2

commit v2 on v1

v2 whole, which is shorter than its diff:
```python
import functools

import jax
import jax.numpy as jnp
from jax import lax
from jax.experimental import pallas as pl
from jax.experimental.pallas import tpu as pltpu
from jax.sharding import PartitionSpec as P

HEADS = 24
HD = 128
TOK = 128
CHUNKS = 3
PART = 4
SPAN = 8
WIDE = 3072
EPS = 1e-05
SCALE = (8 * 32 * 128) ** (-0.5)
MESH = pl.DeviceIdType.MESH
F32 = jnp.float32
BF16 = jnp.bfloat16
GROUP = 4

NN = (((1,), (0,)), ((), ()))
NT = (((1,), (1,)), ((), ()))
TN = (((0,), (0,)), ((), ()))


def mm(a, b, dims):
    return lax.dot_general(a, b, dims, preferred_element_type=F32)


def feature(x):
    return jnp.where(x > 0, x + 1.0, jnp.exp(jnp.minimum(x, 0.0)))


def slope(x):
    return jnp.where(x > 0, 1.0, jnp.exp(jnp.minimum(x, 0.0)))


def cols(h):
    return pl.ds(pl.multiple_of(h * HD, HD), HD)


def kernel(
    x_ref, q_ref, k_ref, v_ref, og_ref,
    dq_out, dk_out, dv_out, dw_out,
    qf, kf, go, ol, dkl, dvl, sc,
    st, pb, cs, r1, rt, rz, ex, pr, po, si,
    dq, dk, dv, kgt, xb, at, cp, xr, zs, zr, tb, tr,
    pair_s, pair_r, in_s, in_r, row_s, row_r, back_s, back_r,
    xb_s, xb_r, at_s, at_r, cx_s, cx_r, z_s, z_r, t_s, t_r, loc,
):
    d = lax.axis_index("dp")
    c = lax.axis_index("ctx")
    y, zh = d // 2, d % 2
    chip, core = c // 2, c % 2
    zl, x = chip // 4, chip % 4
    other = 1 - core

    def dev(y_, zh_, zl_, x_, core_):
        return (y_ * 2 + zh_, (zl_ * 4 + x_) * 2 + core_)

    partner = (d, chip * 2 + other)

    def remote(src, dst, ss, rs, to):
        return pltpu.make_async_remote_copy(
            src_ref=src, dst_ref=dst, send_sem=ss, recv_sem=rs,
            device_id=to, device_id_type=MESH,
        )

    barrier = pltpu.get_barrier_semaphore()

    def greet(to):
        pl.semaphore_signal(barrier, inc=1, device_id=to, device_id_type=MESH)

    greet(partner)
    for o in range(1, 4):
        greet(dev(y, zh, zl, (x + o) % 4, core))
        greet(dev(y, zh, (zl + o) % 4, x, core))
        for cc in (0, 1):
            greet(dev((y + o) % 4, zh, zl, x, cc))
    for o in range(4):
        greet(dev(y, 1 - zh, o, x, core))
    flip = dev(zl, zh, y, x, core)
    off = y != zl

    @pl.when(off)
    def _():
        greet(flip)

    row = lax.broadcasted_iota(jnp.int32, (TOK, TOK), 0)
    col = lax.broadcasted_iota(jnp.int32, (TOK, TOK), 1)
    causal = col <= row

    def heads(k, body):
        def step(g, carry):
            for j in range(GROUP):
                body(SPAN * k + g * GROUP + j)
            return carry

        lax.fori_loop(0, SPAN // GROUP, step, 0)

    def states(h):
        at_h = cols(h)
        kfh = feature(k_ref[:, at_h].astype(F32)).astype(BF16)
        qf[:, at_h] = feature(q_ref[:, at_h].astype(F32)).astype(BF16)
        kf[:, at_h] = kfh
        st[0, h] = mm(kfh, v_ref[:, at_h], TN).astype(BF16)

    def pair_out(s, k):
        return remote(
            st.at[s, pl.ds(SPAN * k + PART * other, PART)], pb.at[s, k],
            pair_s.at[s, 0, k], pair_r.at[s, 0, k], partner,
        )

    def pair_back(s, k, who):
        return remote(
            po.at[s, k], si.at[s, pl.ds(SPAN * k + PART * who, PART)],
            pair_s.at[s, 1, k], pair_r.at[s, 1, k], partner,
        )

    def ahead(o):
        return (x + o) % 4

    def behind(o):
        return (x + 4 - o) % 4

    def x_peer(n):
        return dev(y, zh, zl, n, core)

    def enter(s, k, o, source, slot_, peer):
        return remote(
            cs.at[s, k, source], r1.at[s, k, slot_],
            in_s.at[s, k, o], in_r.at[s, k, o], x_peer(peer),
        )

    def along(s, k, o, slot_, peer):
        return remote(
            rt.at[s, k], rz.at[s, k, slot_],
            row_s.at[s, k, o], row_r.at[s, k, o], dev(y, zh, peer, x, core),
        )

    def leave(s, k, o, source, slot_, peer):
        return remote(
            ex.at[s, k, source], pr.at[s, k, slot_],
            back_s.at[s, k, o], back_r.at[s, k, o], x_peer(peer),
        )

    FAR = (2, 1, 3)

    def stage1(s, k):
        pair_out(s, k).wait_recv()
        for j in range(PART):
            both = st[s, SPAN * k + PART * core + j].astype(F32) + pb[s, k, j].astype(F32)
            cs[s, k, j] = both.astype(BF16)
        for o in FAR:
            enter(s, k, o, ahead(o), x, ahead(o)).start()
        r1[s, k, x] = cs[s, k, x]

    def stage2(s, k):
        for o in (1, 3, 2):
            enter(s, k, o, behind(o), behind(o), behind(o)).wait_recv()
        total = r1[s, k, 0].astype(F32)
        for j in range(1, PART):
            total = total + r1[s, k, j].astype(F32)
        rt[s, k] = total.astype(BF16)
        for o in FAR:
            to = (zl + o) % 4
            along(s, k, o, zl, to).start()
        rz[s, k, zl] = rt[s, k]

    def stage3(s, k):
        for o in (1, 3, 2):
            src = (zl + 4 - o) % 4
            along(s, k, o, src, src).wait_recv()
        total = jnp.zeros((HD, HD), F32)
        for n in range(4):
            counts = (zl > n) if s == 0 else (zl < n)
            total = total + jnp.where(counts, 1.0, 0.0) * rz[s, k, n].astype(F32)
        for j in range(4):
            n = j if s == 0 else 3 - j
            ex[s, k, n] = total.astype(BF16)
            total = total + r1[s, k, n].astype(F32)
        for o in FAR:
            leave(s, k, o, ahead(o), x, ahead(o)).start()
        pr[s, k, x] = ex[s, k, x]

    def stage4(s, k):
        for o in (1, 3, 2):
            leave(s, k, o, behind(o), behind(o), behind(o)).wait_recv()
        mine_on = (core if s == 0 else 1 - core).astype(F32)
        for j in range(PART):
            own = st[s, SPAN * k + PART * core + j].astype(F32)
            po[s, k, j] = (pr[s, k, j].astype(F32) + (1.0 - mine_on) * own).astype(BF16)
        pair_back(s, k, core).start()
        for j in range(PART):
            theirs = pb[s, k, j].astype(F32)
            si[s, SPAN * k + PART * core + j] = (pr[s, k, j].astype(F32) + mine_on * theirs).astype(BF16)

    def stage5(s, k):
        pair_back(s, k, other).wait_recv()

    slot = 2 * y + core

    def xrows(n):
        return pl.ds(pl.multiple_of(TOK * n, TOK), TOK)

    own_x = pltpu.make_async_copy(x_ref, xb.at[xrows(slot)], loc.at[0])

    def x_send(o):
        return remote(
            x_ref, xb.at[xrows(slot)], xb_s.at[o], xb_r.at[o],
            dev((y + o) % 4, zh, zl, x, core),
        )

    def x_in(o):
        src = (y + 4 - o) % 4
        return remote(
            x_ref, xb.at[xrows(2 * src + core)], xb_s.at[o], xb_r.at[o],
            dev(src, zh, zl, x, core),
        )

    def x_pass(o, who):
        rows = xb.at[xrows(2 * ((y + 4 - o) % 4) + who)]
        return remote(rows, rows, xb_s.at[4 + o], xb_r.at[4 + o], partner)

    x_keep = remote(x_ref, xb.at[xrows(slot)], xb_s.at[4], xb_r.at[4], partner)
    x_keep_in = remote(x_ref, xb.at[xrows(2 * y + other)], xb_s.at[4], xb_r.at[4], partner)

    def local_out(h):
        at_h = cols(h)
        s_h = mm(qf[:, at_h], kf[:, at_h], NT)
        s_h = jnp.where(causal, s_h, 0.0).astype(BF16)
        sc[h] = s_h
        ol[:, at_h] = mm(s_h, v_ref[:, at_h], NN)

    def grads(h):
        at_h = cols(h)
        out = ol[:, at_h] + mm(qf[:, at_h], si[0, h], NN)
        inv = lax.rsqrt(jnp.mean(out * out, axis=-1, keepdims=True) + EPS)
        normed = out * inv
        up = og_ref[:, at_h].astype(F32)
        proj = jnp.mean(up * normed, axis=-1, keepdims=True)
        g_h = (inv * (up - normed * proj)).astype(BF16)
        go[:, at_h] = g_h
        st[1, h] = mm(qf[:, at_h], g_h, TN).astype(BF16)

    def local_grads(h):
        at_h = cols(h)
        g_h = go[:, at_h]
        gs = mm(g_h, v_ref[:, at_h], NT)
        gs = jnp.where(causal, gs, 0.0).astype(BF16)
        total = mm(gs, kf[:, at_h], NN) + mm(g_h, si[0, h], NT)
        dq[:, at_h] = (total * slope(q_ref[:, at_h].astype(F32))).astype(BF16)
        dkl[:, at_h] = mm(gs, qf[:, at_h], TN)
        dvl[:, at_h] = mm(sc[h], g_h, TN)

    def last(h):
        at_h = cols(h)
        gi = si[1, h]
        total = dkl[:, at_h] + mm(v_ref[:, at_h], gi, NT)
        total = total * slope(k_ref[:, at_h].astype(F32))
        dk[:, at_h] = total.astype(BF16)
        kgt[pl.ds(pl.multiple_of(h * HD, HD), HD), :] = total.T.astype(BF16)
        dv[:, at_h] = (dvl[:, at_h] + mm(kf[:, at_h], gi, NN)).astype(BF16)

    def begin(k):
        heads(k, states)
        pair_out(0, k).start()

    def middle(k):
        stage5(0, k)
        heads(k, grads)
        pair_out(1, k).start()

    def end(k):
        stage5(1, k)
        heads(k, last)

    heads(0, states)
    pl.semaphore_wait(barrier, 17 + ((y - zl) * (y - zl) + 8) // 9)
    pair_out(0, 0).start()
    own_x.start()
    for o in FAR:
        x_send(o).start()
    begin(1)
    stage1(0, 0)
    begin(2)
    stage1(0, 1)
    stage1(0, 2)
    x_keep.start()
    heads(0, local_out)
    stage2(0, 0)
    heads(1, local_out)
    stage2(0, 1)
    heads(2, local_out)
    stage2(0, 2)
    stage3(0, 0)
    stage3(0, 1)
    stage4(0, 0)
    stage3(0, 2)
    stage4(0, 1)
    middle(0)
    stage4(0, 2)
    stage1(1, 0)
    middle(1)
    stage1(1, 1)
    stage2(1, 0)
    middle(2)
    stage1(1, 2)
    stage2(1, 1)
    heads(0, local_grads)
    stage3(1, 0)
    stage2(1, 2)
    heads(1, local_grads)
    stage3(1, 1)
    stage4(1, 0)
    stage3(1, 2)
    heads(2, local_grads)
    for o in (1, 3, 2):
        x_in(o).wait_recv()
        x_pass(o, core).start()
    out_q = pltpu.make_async_copy(dq, dq_out, loc.at[1])
    out_q.start()
    stage4(1, 1)
    end(0)
    stage4(1, 2)
    end(1)
    end(2)

    def at_rows(y_, core_, n):
        return kgt.at[pl.ds(pl.multiple_of(768 * y_ + 192 * n + 96 * core_, 96), 96)]

    def at_put(src, n):
        return at.at[pl.ds(96 * n, 96), pl.ds(pl.multiple_of(TOK * src, TOK), TOK)]

    def at_send(o, cc, n):
        y_ = (y + o) % 4
        cc_ = (core + cc) % 2
        return remote(
            at_rows(y_, cc_, n), at_put(slot, n), at_s.at[2 * o + cc, n], at_r.at[2 * o + cc, n],
            dev(y_, zh, zl, x, cc_),
        )

    def at_in(o, cc, n):
        y_ = (y + 4 - o) % 4
        cc_ = (core + cc) % 2
        return remote(
            at_rows(y, core, n), at_put(2 * y_ + cc_, n), at_s.at[2 * o + cc, n], at_r.at[2 * o + cc, n],
            dev(y_, zh, zl, x, cc_),
        )

    peers = [(o, cc) for o in (2, 1, 3, 0) for cc in (0, 1) if (o, cc) != (0, 0)]
    for o, cc in peers:
        for n in range(4):
            at_send(o, cc, n).start()
    for n in range(4):
        keep = pltpu.make_async_copy(at_rows(y, core, n), at_put(slot, n), loc.at[4 + n])
        keep.start()
    out_k = pltpu.make_async_copy(dk, dk_out, loc.at[2])
    out_v = pltpu.make_async_copy(dv, dv_out, loc.at[3])
    out_k.start()
    out_v.start()

    own_x.wait()
    x_keep_in.wait_recv()
    for o in (1, 3, 2):
        x_pass(o, other).wait_recv()
    for n in range(4):
        pltpu.make_async_copy(at_rows(y, core, n), at_put(slot, n), loc.at[4 + n]).wait()
        for o, cc in peers:
            at_in(o, cc, n).wait_recv()

    z = zh * 4 + zl

    def cx_send(o, n):
        return remote(cp.at[n, ahead(o)], xr.at[n, x], cx_s.at[o, n], cx_r.at[o, n], x_peer(ahead(o)))

    def cx_in(o, n):
        return remote(cp.at[n, behind(o)], xr.at[n, behind(o)], cx_s.at[o, n], cx_r.at[o, n], x_peer(behind(o)))

    def product(n, carry):
        to = (z + 1 + n) % 8
        tile = (to % 4) * 2 + to // 4
        out = mm(at[...], xb[:, pl.ds(pl.multiple_of(tile * 384, 384), 384)], NN).astype(BF16)
        for i in range(4):
            cp[n, i] = out[96 * i:96 * (i + 1), :]
        for o in FAR:
            cx_send(o, n).start()
        return carry

    lax.fori_loop(0, 8, product, 0)

    def z_send(n):
        to = (z + 1 + n) % 8
        return remote(
            zs.at[n], zr.at[n], z_s.at[n], z_r.at[n], dev(y, to // 4, to % 4, x, core),
        )

    def z_in(n):
        src = (z + 7 - n) % 8
        return remote(
            zs.at[n], zr.at[n], z_s.at[n], z_r.at[n], dev(y, src // 4, src % 4, x, core),
        )

    def sum_x(n):
        for o in (1, 3, 2):
            cx_in(o, n).wait_recv()
        total = cp[n, x].astype(F32)
        for o in range(1, 4):
            total = total + xr[n, (x + o) % 4].astype(F32)
        return total

    def relay(n, carry):
        zs[n] = sum_x(n).astype(BF16)
        z_send(n).start()
        return carry

    lax.fori_loop(0, 7, relay, 0)
    total = sum_x(7)
    for n in range(7):
        z_in(n).wait_recv()
        total = total + zr[n].astype(F32)
    tb[...] = total.astype(BF16)

    turn = remote(tb, tr, t_s.at[0], t_r.at[0], flip)

    @pl.when(off)
    def _():
        turn.start()
        turn.wait()
        dw_out[...] = tr[...].astype(F32) * SCALE

    @pl.when(jnp.logical_not(off))
    def _():
        dw_out[...] = tb[...].astype(F32) * SCALE

    for s in (0, 1):
        for k in range(CHUNKS):
            pair_out(s, k).wait_send()
            pair_back(s, k, core).wait_send()
            for o in FAR:
                enter(s, k, o, ahead(o), x, ahead(o)).wait_send()
                along(s, k, o, zl, (zl + o) % 4).wait_send()
                leave(s, k, o, ahead(o), x, ahead(o)).wait_send()
    for o in FAR:
        x_send(o).wait_send()
        x_pass(o, core).wait_send()
        for n in range(8):
            cx_send(o, n).wait_send()
    x_keep.wait_send()
    for o, cc in peers:
        for n in range(4):
            at_send(o, cc, n).wait_send()
    for n in range(7):
        z_send(n).wait_send()
    out_q.wait()
    out_k.wait()
    out_v.wait()


def hand_on(*refs):
    count = len(refs) // 2
    for source, target in zip(refs[:count], refs[count:]):
        target[...] = source[...]


def shards(layer_input, query_rows, key_rows, value_rows, out_grad):
    vmem = pl.BlockSpec(memory_space=pltpu.VMEM)
    hbm = pl.BlockSpec(memory_space=pl.ANY)
    rows = (TOK, WIDE)
    steps = (2, CHUNKS)
    square = (HD, HD)
    dma = pltpu.SemaphoreType.DMA
    dq, dk, dv, dw = pl.pallas_call(
        kernel,
        out_shape=(
            jax.ShapeDtypeStruct(rows, BF16),
            jax.ShapeDtypeStruct(rows, BF16),
            jax.ShapeDtypeStruct(rows, BF16),
            jax.ShapeDtypeStruct((96, 384), F32),
        ),
        in_specs=[hbm, vmem, vmem, vmem, vmem],
        out_specs=(hbm, hbm, hbm, vmem),
        scratch_shapes=[
            pltpu.VMEM(rows, BF16),
            pltpu.VMEM(rows, BF16),
            pltpu.VMEM(rows, BF16),
            pltpu.VMEM(rows, F32),
            pltpu.VMEM(rows, F32),
            pltpu.VMEM(rows, F32),
            pltpu.VMEM((HEADS, HD, HD), BF16),
            pltpu.VMEM((2, HEADS, HD, HD), BF16),
            pltpu.VMEM(steps + (PART,) + square, BF16),
            pltpu.VMEM(steps + (PART,) + square, BF16),
            pltpu.VMEM(steps + (PART,) + square, BF16),
            pltpu.VMEM(steps + square, BF16),
            pltpu.VMEM(steps + (PART,) + square, BF16),
            pltpu.VMEM(steps + (PART,) + square, BF16),
            pltpu.VMEM(steps + (PART,) + square, BF16),
            pltpu.VMEM(steps + (PART,) + square, BF16),
            pltpu.VMEM((2, HEADS, HD, HD), BF16),
            pltpu.VMEM(rows, BF16),
            pltpu.VMEM(rows, BF16),
            pltpu.VMEM(rows, BF16),
            pltpu.VMEM((WIDE, TOK), BF16),
            pltpu.VMEM((8 * TOK, WIDE), BF16),
            pltpu.VMEM((384, 8 * TOK), BF16),
            pltpu.VMEM((8, 4, 96, 384), BF16),
            pltpu.VMEM((8, 4, 96, 384), BF16),
            pltpu.VMEM((8, 96, 384), BF16),
            pltpu.VMEM((8, 96, 384), BF16),
            pltpu.VMEM((96, 384), BF16),
            pltpu.VMEM((96, 384), BF16),
            dma((2, 2, CHUNKS)), dma((2, 2, CHUNKS)),
            dma(steps + (4,)), dma(steps + (4,)),
            dma(steps + (4,)), dma(steps + (4,)),
            dma(steps + (4,)), dma(steps + (4,)),
            dma((8,)), dma((8,)),
            dma((8, 4)), dma((8, 4)),
            dma((4, 8)), dma((4, 8)),
            dma((8,)), dma((8,)),
            dma((1,)), dma((1,)),
            dma((8,)),
        ],
        compiler_params=pltpu.CompilerParams(
            collective_id=0, has_side_effects=True, vmem_limit_bytes=60 * 1024 * 1024
        ),
    )(layer_input[0], query_rows[0], key_rows[0], value_rows[0], out_grad[0])
    blocks = [pl.BlockSpec((32, WIDE), lambda i: (i, 0))] * 3 + [pl.BlockSpec((24, 384), lambda i: (i, 0))]
    arrays = (dq, dk, dv, dw)
    dq, dk, dv, dw = pl.pallas_call(
        hand_on,
        out_shape=tuple(jax.ShapeDtypeStruct(a.shape, a.dtype) for a in arrays),
        grid=(4,),
        in_specs=blocks,
        out_specs=tuple(blocks),
    )(*arrays)
    return dq[None], dk[None], dv[None], dw


def solution(mesh):
    placed = (P("dp", "ctx", None),) * 5
    return jax.shard_map(
        shards,
        mesh=mesh,
        in_specs=placed,
        out_specs=(
            P("dp", "ctx", None),
            P("dp", "ctx", None),
            P("dp", "ctx", None),
            P("ctx", "dp"),
        ),
        check_vma=False,
    )
```

time: 138 us -> 112 us (0.81)
  Pallas kernels: 132 us -> 111 us
  local copies, waits for them, and re-layouts: 5.24 us -> 0 us
    pallas_call x1, Pallas kernels: 132 us -> 107 us  [shards(): pl.pallas_call(kernel, out_shape=(jax.ShapeDtypeStruct(rows, BF16), jax.S...]
    unnamed x10 -> x0, local copies, waits for them, and re-layouts: 5.24 us -> none
    pallas_call x0 -> x1, Pallas kernels: none -> 3.93 us  [shards(): pl.pallas_call(hand_on, out_shape=tuple((jax.ShapeDtypeStruct(a.shape, a....]
where the time goes in v2:
time: 112 us; the launch traced here: 111 us
  Pallas kernels  111 us (99%)
    pallas_call x1, Pallas kernels, shards(): pl.pallas_call(kernel, out_shape=(jax.ShapeDtypeStruct(rows, BF16), jax.S...  107 us
    pallas_call x1, Pallas kernels, shards(): pl.pallas_call(hand_on, out_shape=tuple((jax.ShapeDtypeStruct(a.shape, a....  3.93 us

profile of v2, /device:TPU:8, one launch (start us, length us, event | category | flops | bytes accessed | tf_op | source)
XLA Modules:
  0.0 111.4 jit_solution(15923422934846779068)
XLA Ops:
  0.6 106.9 %shard_map.84 = (bf16[128,3072]{1,0:T(8,128)(2,1)}, bf16[128,3072]{1,0:T(8,128)(2,1)}, bf16[128,3072]{1,0:T(8,128)(2,1)}, f32[96,384]{1,0:T(8,128)}) custom-call(bf16[128,3072]{1,0:T(8,128)(2,1)} %bitcast.8, bf16[128,3072]{1,0:T(8,128)(2,1)} %bitcast.9, bf16[128,3072]{1,0:T(8,128)(2,1)} %bitcast.10, bf16[128,3072]{1,0:T(8,128)(2,1)} %bitcast.11, ...), custom_call_target="tpu_custom_call" | custom-call | tf_op jit(solution)/shard_map/pallas_call | solution.py:476
  107.5 3.9 %shard_map.85 = (bf16[128,3072]{1,0:T(8,128)(2,1)}, bf16[128,3072]{1,0:T(8,128)(2,1)}, bf16[128,3072]{1,0:T(8,128)(2,1)}, f32[96,384]{1,0:T(8,128)}) custom-call(bf16[128,3072]{1,0:T(8,128)(2,1)} %get-tuple-element.12.refs_0_, bf16[128,3072]{1,0:T(8,128)(2,1)} %get-tuple-element.13.refs_1_, bf16[128,3072]{1,0:T(8,128)(2,1)} %get-tuple-element.14.refs_2_, ...), custom_call_target="tpu_custom_call" | custom-call | tf_op jit(solution)/shard_map/pallas_call | solution.py:533
